TPU v7x, 32 devices: a whole 2x2x4 slice. The times are simulated.
32 devices in a mesh: chan: 4 (over x, core), slab: 8 (over z, y).
Axes of the slice: x: 2, y: 2, z: 4, core: 2. Of those that a mesh axis runs over, the one named last changes fastest.
Arguments:
- image: float32 [4, 1024, 1024], P('chan', 'slab'), may hold values from 0 to 2
- margin: int32 [8], P('slab'), may hold values from 1 to 3
- cells: int32 [4, 32768], P('chan', 'slab'), may hold values from 1 to 131071
- weights: float32 [4, 32768], P('chan', 'slab'), may hold values from 0.25 to 4
- observed: float32 [2, 4, 32768], P(None, 'chan', 'slab'), may hold values from -6 to 6
- dual_start: float32 [2, 4, 32768], P(None, 'chan', 'slab'), may hold values from -4 to 4
Outputs:
- restored: float32 [4, 1024, 1024], P('chan', 'slab')
- vis_dual: float32 [2, 4, 32768], P(None, 'chan', 'slab')
Inputs may be any that keep to these rules, and one draw needn't show every extreme that they name: `cells`: visibility k of a channel belongs to facet s = k div 4096; its value q names frequency column s * 128 + q div 1024 and frequency row q mod 1024.
All inputs are finite; a program needn't handle non-finite values.
Results may differ from a plain program's by a relative error of at most 0.0047.
Values may be sent and summed in bfloat16 or wider, within the bound.
A program may use at most 64 MiB of HBM per device.

v0:
```python
import math

import jax
import jax.numpy as jnp
from jax import lax
from jax.sharding import PartitionSpec as P

N = 1024
HALO = 3


low_taps = (
    -0.010597401784997278,
    0.032883011666982945,
    0.030841381835986965,
    -0.18703481171888114,
    -0.02798376941698385,
    0.6308807679295904,
    0.7148465705525415,
    0.23037781330885523,
)
high_taps = (
    -0.23037781330885523,
    0.7148465705525415,
    -0.6308807679295904,
    -0.02798376941698385,
    0.18703481171888114,
    0.030841381835986965,
    -0.032883011666982945,
    -0.010597401784997278,
)
tau_step = 0.5
bound_level = 3.0
leading = (((0,), (0,)), ((), ()))


def with_halo(block, sides, width):
    for axis, dim in sides:
        count = lax.axis_size(axis)
        forward = [(i, i + 1) for i in range(count - 1)]
        backward = [(target, source) for source, target in forward]
        low = lax.ppermute(
            lax.slice_in_dim(block, block.shape[dim] - width, None, axis=dim), axis, forward
        )
        high = lax.ppermute(lax.slice_in_dim(block, 0, width, axis=dim), axis, backward)
        block = jnp.concatenate([low, block, high], axis=dim)
    return block


def tap_value(offset, taps):
    total = jnp.zeros(offset.shape, jnp.float32)
    for position in range(8):
        total = total + jnp.where(offset == position, taps[position], 0.0).astype(jnp.float32)
    return total


def fourier_tables(length):
    index = jnp.arange(length, dtype=jnp.int32)
    product = index[:, None] * index[None, :] % length
    angle = product.astype(jnp.float32) * (2.0 * math.pi / length)
    scale = 1.0 / math.sqrt(length)
    return (
        (jnp.cos(angle) * scale).astype(jnp.bfloat16),
        (jnp.sin(angle) * scale).astype(jnp.bfloat16),
    )


def row_matrix(count):
    half = count // 2
    line = jnp.arange(count + 2 * HALO, dtype=jnp.int32)[:, None]
    column = jnp.arange(count, dtype=jnp.int32)[None, :]
    offset = line - 2 * (column % half)
    return jnp.where(column < half, tap_value(offset, low_taps), tap_value(offset, high_taps))


def facet_mask(count, width):
    line = jnp.arange(count + 2 * HALO, dtype=jnp.int32)
    distance = jnp.maximum(jnp.maximum(HALO - line, line - count - HALO + 1), 0)
    return (distance[None, :] <= width[:, None]).astype(jnp.float32)


def column_forward(values):
    width = values.shape[1]
    half = width // 2
    padded = jnp.pad(values, ((0, 0), (HALO, 8)))
    even_cells = padded[:, 0::2]
    odd_cells = padded[:, 1::2]
    low_part = jnp.zeros((values.shape[0], half), jnp.float32)
    high_part = jnp.zeros((values.shape[0], half), jnp.float32)
    for position in range(8):
        source = even_cells if position % 2 == 0 else odd_cells
        piece = source[:, position // 2 : position // 2 + half]
        low_part = low_part + low_taps[position] * piece
        high_part = high_part + high_taps[position] * piece
    return jnp.concatenate([low_part, high_part], axis=1)


def column_adjoint(coefs):
    width = coefs.shape[1]
    half = width // 2
    low_part = coefs[:, :half]
    high_part = coefs[:, half:]
    even_sums = jnp.zeros((coefs.shape[0], half + 4), jnp.float32)
    odd_sums = jnp.zeros((coefs.shape[0], half + 4), jnp.float32)
    for position in range(8):
        term = low_taps[position] * low_part + high_taps[position] * high_part
        placed = jnp.pad(term, ((0, 0), (position // 2, 4 - position // 2)))
        if position % 2 == 0:
            even_sums = even_sums + placed
        else:
            odd_sums = odd_sums + placed
    joined = jnp.stack([even_sums, odd_sums], axis=2).reshape(coefs.shape[0], width + 8)
    return joined[:, HALO : HALO + width]


def data_part(lifted, dual, seen, places, gains, cos_table, sin_table):
    flat_b = lifted.astype(jnp.bfloat16)
    spectra = jnp.stack(
        [
            jnp.dot(flat_b, cos_table, preferred_element_type=jnp.float32),
            -jnp.dot(flat_b, sin_table, preferred_element_type=jnp.float32),
        ]
    ).astype(jnp.bfloat16)
    columns = lax.all_to_all(spectra, "slab", split_axis=2, concat_axis=1, tiled=True)
    grid_real = lax.dot_general(
        columns[0], cos_table, leading, preferred_element_type=jnp.float32
    ) + lax.dot_general(columns[1], sin_table, leading, preferred_element_type=jnp.float32)
    grid_imag = lax.dot_general(
        columns[1], cos_table, leading, preferred_element_type=jnp.float32
    ) - lax.dot_general(columns[0], sin_table, leading, preferred_element_type=jnp.float32)
    model = jnp.stack(
        [gains * grid_real.reshape(-1)[places], gains * grid_imag.reshape(-1)[places]]
    )
    fresh_dual = (dual + (model - seen)) / 2.0
    weighted = gains[None, :] * fresh_dual
    cell_count = grid_real.size
    hold_real = (
        jnp.zeros((cell_count,), jnp.float32)
        .at[places]
        .add(weighted[0])
        .reshape(grid_real.shape)
        .astype(jnp.bfloat16)
    )
    hold_imag = (
        jnp.zeros((cell_count,), jnp.float32)
        .at[places]
        .add(weighted[1])
        .reshape(grid_real.shape)
        .astype(jnp.bfloat16)
    )
    backward = jnp.stack(
        [
            jnp.dot(hold_real, cos_table, preferred_element_type=jnp.float32)
            - jnp.dot(hold_imag, sin_table, preferred_element_type=jnp.float32),
            jnp.dot(hold_real, sin_table, preferred_element_type=jnp.float32)
            + jnp.dot(hold_imag, cos_table, preferred_element_type=jnp.float32),
        ]
    ).astype(jnp.bfloat16)
    returned = lax.all_to_all(backward, "slab", split_axis=2, concat_axis=1, tiled=True)
    data_term = lax.dot_general(
        returned[0], cos_table, leading, preferred_element_type=jnp.float32
    ) - lax.dot_general(returned[1], sin_table, leading, preferred_element_type=jnp.float32)
    return (data_term, fresh_dual)


def wave_part(lifted, row_map, mask):
    highest = lax.Precision.HIGHEST
    count = lifted.shape[0]
    extended = with_halo(lifted, (("slab", 0),), HALO) * mask
    filtered = column_forward(extended)
    coef = lax.dot_general(
        row_map, filtered, leading, precision=highest, preferred_element_type=jnp.float32
    )
    squares = coef * coef
    share = lax.psum_scatter(
        squares.astype(jnp.bfloat16), "chan", scatter_dimension=1, tiled=True
    ).astype(jnp.float32)
    partial_factor = bound_level / jnp.maximum(jnp.sqrt(share), bound_level)
    factor = lax.all_gather(partial_factor, "chan", axis=1, tiled=True)
    fresh_dual = coef * factor
    back = column_adjoint(fresh_dual)
    spread = jnp.dot(row_map, back, precision=highest, preferred_element_type=jnp.float32) * mask
    bands = jnp.concatenate([spread[:HALO], spread[count + HALO :]], axis=0)
    arrived = with_halo(bands, (("slab", 0),), HALO)
    inner = spread[HALO : count + HALO]
    inner = inner.at[:HALO].add(arrived[:HALO])
    inner = inner.at[count - HALO :].add(arrived[3 * HALO :])
    return (inner, fresh_dual)


def local(image, margin, cells, weights, observed, dual_start):
    count = image.shape[1]
    cos_table, sin_table = fourier_tables(N)
    row_map = row_matrix(count)
    mask = facet_mask(count, margin)[0][:, None]
    places = cells[0]
    gains = weights[0]
    seen = observed[:, 0, :]
    dual = dual_start[:, 0, :]
    estimate = image[0]
    data_term, dual = data_part(estimate, dual, seen, places, gains, cos_table, sin_table)
    wave_term, wave_dual = wave_part(estimate, row_map, mask)
    fresh = jnp.maximum(estimate - tau_step * (data_term + wave_term), 0.0)
    return (fresh[None], dual[:, None, :])


def solution(mesh):
    in_specs = (
        P("chan", "slab", None),
        P("slab"),
        P("chan", "slab"),
        P("chan", "slab"),
        P(None, "chan", "slab"),
        P(None, "chan", "slab"),
    )
    out_specs = (P("chan", "slab", None), P(None, "chan", "slab"))
    return jax.shard_map(local, mesh=mesh, in_specs=in_specs, out_specs=out_specs, check_vma=False)
```

profile of v0, /device:TPU:0, one launch (start us, length us, event | category | flops | bytes accessed | tf_op | source)
XLA Modules:
  0.0 399.8 jit_solution(13848005929283829801)
XLA Ops:
  7.2 0.8 slice_bitcast_fusion.1
  7.9 1.3 collective-permute-start.1
  9.2 5.7 %collective-permute-start = (f32[3,1024]{1,0:T(4,128)S(1)}, f32[3,1024]{1,0:T(4,128)S(1)}, u32[]{:S(2)}, u32[]{:S(2)}) collective-permute-start(f32[3,1024]{1,0:T(4,128)S(1)} %get-tuple-element.42), channel_id=1, source_target_pairs={{0,1},{1,2},{2,3},{3,4},{4,5},{5,6},{6,7},{8,9},{9,10},{10,11},{11... | collective-permute-start | bytes 36872 | tf_op jit(solution)/shard_map/ppermute | solution.py:42
  14.9 17.0 %fusion.38 = bf16[1,128,1024]{1,2,0:T(8,128)(2,1)S(1)} fusion(f32[1,128,1024]{2,1,0:T(8,128)} %param.10), kind=kOutput, calls=%fused_computation.48 | convolution fusion | flops 285474816 | bytes 786432 | tf_op jit(solution)/shard_map/dot_general | solution.py:121
  32.0 16.0 %fusion.37 = bf16[1,128,1024]{1,2,0:T(8,128)(2,1)S(1)} fusion(f32[1,128,1024]{2,1,0:T(8,128)S(1)} %copy-done), kind=kOutput, calls=%fused_computation.47 | convolution fusion | flops 285212672 | bytes 786432 | tf_op jit(solution)/shard_map/dot_general | solution.py:120
  48.1 1.3 copy.14
  49.4 6.2 %all-to-all-start = ((bf16[2,128,1024]{1,0,2:T(2,128)(2,1)}), bf16[2,128,1024]{1,0,2:T(2,128)(2,1)S(1)}, u32[]{:S(2)}, u32[]{:S(2)}) async-start(bf16[2,128,1024]{1,0,2:T(2,128)(2,1)} %copy.14), calls=%async_computation | async-start | bytes 1048576 | tf_op jit(solution)/shard_map/all_to_all | solution.py:124
  56.7 10.4 %slice.135 = f32[134,517]{1,0:T(8,128)S(1)} slice(f32[134,1035]{1,0:T(8,128)S(1)} %pad.36), slice={[0:134:1], [1:1035:2]} | slice | bytes 554224 | tf_op jit(solution)/shard_map/slice | solution.py:87
  67.1 10.2 %slice.133 = f32[134,518]{1,0:T(8,128)S(1)} slice(f32[134,1035]{1,0:T(8,128)S(1)} %pad.36), slice={[0:134:1], [0:1035:2]} | slice | bytes 555296 | tf_op jit(solution)/shard_map/slice | solution.py:86
  77.8 1.4 multiply_convert_fusion.56
  79.2 21.5 %reduce-scatter.2.cloned.1.call-done = bf16[128,256]{1,0:T(8,128)(2,1)} async-done(((bf16[128,1024]{1,0:T(8,128)(2,1)}), bf16[128,256]{1,0:T(8,128)(2,1)}) %reduce-scatter.2.cloned.1.call-update) | async-done | bytes 65552 | tf_op jit(solution)/shard_map/reduce_scatter | solution.py:175
  100.8 0.9 maximum_divide_fusion
  101.7 6.5 %all_gather.3 = f32[128,1024]{1,0:T(8,128)S(1)} all-gather(f32[128,256]{1,0:T(8,128)S(1)} %maximum_divide_fusion), channel_id=1, replica_groups=mesh['chan'=4,'slab'=8] {'chan'}, dimensions={1}, use_global_device_ids=true | all-gather | bytes 655360 | tf_op jit(solution)/shard_map/all_gather | solution.py:179
  110.2 3.4 collective-permute-start.2
  113.7 1.3 collective-permute-start.3
  116.1 16.1 %fusion.10 = f32[128,1024]{1,0:T(8,128)S(1)} fusion(bf16[1024,128]{1,0:T(8,128)(2,1)S(1)} %bitcast.99), kind=kOutput, calls=%fused_computation.19 | convolution fusion | flops 285212672 | bytes 786432 | tf_op jit(solution)/shard_map/dot_general | solution.py:125
  132.3 16.1 %fusion.9 = f32[128,1024]{1,0:T(8,128)S(1)} fusion(bf16[1024,128]{1,0:T(8,128)(2,1)S(1)} %bitcast.101), kind=kOutput, calls=%fused_computation.18 | convolution fusion | flops 285212672 | bytes 786432 | tf_op jit(solution)/shard_map/dot_general | solution.py:128
  148.4 16.4 %fusion.19 = f32[16,8,8,128]{3,2,1,0:T(8,128)S(1)} fusion(f32[128,1024]{1,0:T(8,128)S(1)} %fusion.10, bf16[1024,128]{1,0:T(8,128)(2,1)S(1)} %bitcast.102), kind=kOutput, calls=%fused_computation.29 | convolution fusion | flops 285343744 | bytes 1310720 | tf_op jit(solution)/shard_map/dot_general | solution.py:127
  164.9 16.2 %fusion.21 = f32[16,8,8,128]{3,2,1,0:T(8,128)S(1)} fusion(f32[128,1024]{1,0:T(8,128)S(1)} %fusion.9, bf16[1024,128]{1,0:T(8,128)(2,1)S(1)} %bitcast.100), kind=kOutput, calls=%fused_computation.31 | convolution fusion | flops 285343744 | bytes 1310720 | tf_op jit(solution)/shard_map/dot_general | solution.py:130
  181.3 23.0 %gather_fusion = f32[4096]{0:T(1024)S(1)} fusion(f32[131072]{0:T(1024)S(1)} %bitcast.93, s32[4096]{0:T(1024)S(1)} %broadcast_clamp_fusion), kind=kCustom, calls=%fused_computation | custom fusion | bytes 49152 | tf_op jit(solution)/shard_map/gather | solution.py:132
  204.3 23.0 %gather_fusion.1 = f32[4096]{0:T(1024)S(1)} fusion(f32[131072]{0:T(1024)S(1)} %bitcast.94, s32[4096]{0:T(1024)S(1)} %broadcast_clamp_fusion), kind=kCustom, calls=%fused_computation.1 | custom fusion | bytes 49152 | tf_op jit(solution)/shard_map/gather | solution.py:132
  227.6 22.0 %scatter_custom_fusion.1 = f32[131072]{0:T(1024)S(1)} fusion(s32[4096]{0:T(1024)S(1)} %bitcast.108, f32[4096]{0:T(1024)S(1)} %bitcast.114, f32[]{:T(128)} %constant.146.clone.1), kind=kCustom, calls=%fused_computation.71 | custom fusion | flops 4096 | bytes 524292 | tf_op jit(solution)/shard_map/scatter-add | solution.py:147
  249.8 16.5 %fusion.7 = f32[128,1024]{1,0:T(8,128)S(1)} fusion(bf16[128,1024]{1,0:T(8,128)(2,1)S(1)} %convert_element_type.104), kind=kOutput, calls=%fused_computation.16 | convolution fusion | flops 285212672 | bytes 786432 | tf_op jit(solution)/shard_map/dot_general | solution.py:156
  266.3 22.0 %scatter_custom_fusion = f32[131072]{0:T(1024)S(1)} fusion(s32[4096]{0:T(1024)S(1)} %bitcast.109, f32[4096]{0:T(1024)S(1)} %bitcast.113, f32[]{:T(128)} %constant.146.clone.1), kind=kCustom, calls=%fused_computation.73 | custom fusion | flops 4096 | bytes 524292 | tf_op jit(solution)/shard_map/scatter-add | solution.py:140
  288.5 16.1 %fusion.8 = f32[128,1024]{1,0:T(8,128)S(1)} fusion(bf16[128,1024]{1,0:T(8,128)(2,1)S(1)} %convert_element_type.102), kind=kOutput, calls=%fused_computation.17 | convolution fusion | flops 285212672 | bytes 786432 | tf_op jit(solution)/shard_map/dot_general | solution.py:153
  304.5 16.2 %fusion.36 = bf16[1,128,1024]{2,1,0:T(8,128)(2,1)S(1)} fusion(f32[128,1024]{1,0:T(8,128)S(1)} %fusion.7, bf16[128,1024]{1,0:T(8,128)(2,1)S(1)} %convert_element_type.102), kind=kOutput, calls=%fused_computation.46 | convolution fusion | flops 285474816 | bytes 1048576 | tf_op jit(solution)/shard_map/dot_general | solution.py:155
  320.7 16.4 %fusion.35 = bf16[1,128,1024]{2,1,0:T(8,128)(2,1)S(1)} fusion(f32[128,1024]{1,0:T(8,128)S(1)} %fusion.8, bf16[128,1024]{1,0:T(8,128)(2,1)S(1)} %convert_element_type.104), kind=kOutput, calls=%fused_computation.45 | convolution fusion | flops 285474816 | bytes 1048576 | tf_op jit(solution)/shard_map/dot_general | solution.py:154
  337.1 1.1 copy.18
  338.3 6.6 %all-to-all-start.1 = ((bf16[2,128,1024]{1,0,2:T(2,128)(2,1)}), bf16[2,128,1024]{1,0,2:T(2,128)(2,1)S(1)}, u32[]{:S(2)}, u32[]{:S(2)}) async-start(bf16[2,128,1024]{1,0,2:T(2,128)(2,1)} %copy.18), calls=%async_computation.1 | async-start | bytes 1048576 | tf_op jit(solution)/shard_map/all_to_all | solution.py:159
  345.8 13.5 %all-to-all-done.1 = bf16[2,128,1024]{1,0,2:T(2,128)(2,1)S(1)} async-done(((bf16[2,128,1024]{1,0,2:T(2,128)(2,1)}), bf16[2,128,1024]{1,0,2:T(2,128)(2,1)S(1)}, u32[]{:S(2)}, u32[]{:S(2)}) %all-to-all-start.1) | async-done | bytes 524320 | tf_op jit(solution)/shard_map/all_to_all | solution.py:159
  359.6 16.1 %fusion.6 = f32[128,1024]{1,0:T(8,128)S(1)} fusion(bf16[1024,128]{1,0:T(8,128)(2,1)S(1)} %bitcast.104), kind=kOutput, calls=%fused_computation.15 | convolution fusion | flops 285212672 | bytes 786432 | tf_op jit(solution)/shard_map/dot_general | solution.py:160
  375.9 16.9 %fusion.29 = f32[1,128,1024]{2,1,0:T(8,128)} fusion(f32[128,1024]{1,0:T(8,128)S(1)} %scatter-add.27, f32[128,1024]{1,0:T(8,128)S(1)} %fusion.6, bf16[1024,128]{1,0:T(8,128)(2,1)S(1)} %bitcast.103, f32[1,128,1024]{2,1,0:T(8,128)S(1)} %copy-done), kind=kOutput, calls=%fused_computation.39 | convolution fusion | flops 285868032 | bytes 2359296 | tf_op jit(solution)/shard_map/dot_general | solution.py:162
  (57 shorter events, 6.3 us)
Async XLA Ops:
  7.9 48.4 %collective-permute-start.1 = (f32[3,1024]{1,0:T(4,128)S(1)}, f32[3,1024]{1,0:T(4,128)S(1)}, u32[]{:S(2)}, u32[]{:S(2)}) collective-permute-start(f32[3,1024]{1,0:T(4,128)S(1)} %get-tuple-element.43), channel_id=1, source_target_pairs={{1,0},{2,1},{3,2},{4,3},{5,4},{6,5},{7,6},{9,8},{10,9},{11,10},{12... | collective-permute-start | bytes 36872 | tf_op jit(solution)/shard_map/ppermute | solution.py:45
  9.2 22.7 %copy-start = (f32[1,128,1024]{2,1,0:T(8,128)S(1)}, f32[1,128,1024]{2,1,0:T(8,128)}, u32[]{:S(2)}) copy-start(f32[1,128,1024]{2,1,0:T(8,128)} %param.10) | copy-start | bytes 1572868
  9.2 47.1 %collective-permute-start = (f32[3,1024]{1,0:T(4,128)S(1)}, f32[3,1024]{1,0:T(4,128)S(1)}, u32[]{:S(2)}, u32[]{:S(2)}) collective-permute-start(f32[3,1024]{1,0:T(4,128)S(1)} %get-tuple-element.42), channel_id=1, source_target_pairs={{0,1},{1,2},{2,3},{3,4},{4,5},{5,6},{6,7},{8,9},{9,10},{10,11},{11... | collective-permute-start | bytes 36872 | tf_op jit(solution)/shard_map/ppermute | solution.py:42
  49.4 66.4 %all-to-all-start = ((bf16[2,128,1024]{1,0,2:T(2,128)(2,1)}), bf16[2,128,1024]{1,0,2:T(2,128)(2,1)S(1)}, u32[]{:S(2)}, u32[]{:S(2)}) async-start(bf16[2,128,1024]{1,0,2:T(2,128)(2,1)} %copy.14), calls=%async_computation | async-start | bytes 1048576 | tf_op jit(solution)/shard_map/all_to_all | solution.py:124
  55.6 45.1 %reduce-scatter.2.cloned.1.call-start = ((), (), s32[]{:S(2)}) async-start(), calls=%async_computation.3 | async-start | bytes 327680 | tf_op jit(solution)/shard_map/reduce_scatter | solution.py:175
  77.8 1.4 copy-start.3
  110.2 4.8 %collective-permute-start.2 = (f32[3,1024]{1,0:T(4,128)S(1)}, f32[3,1024]{1,0:T(4,128)S(1)}, u32[]{:S(2)}, u32[]{:S(2)}) collective-permute-start(f32[3,1024]{1,0:T(4,128)S(1)} %get-tuple-element.29), channel_id=1, source_target_pairs={{0,1},{1,2},{2,3},{3,4},{4,5},{5,6},{6,7},{8,9},{9,10},{10,11},{11... | collective-permute-start | bytes 36872 | tf_op jit(solution)/shard_map/ppermute | solution.py:42
  113.7 231.2 %collective-permute-start.3 = (f32[3,1024]{1,0:T(4,128)S(1)}, f32[3,1024]{1,0:T(4,128)S(1)}, u32[]{:S(2)}, u32[]{:S(2)}) collective-permute-start(f32[3,1024]{1,0:T(4,128)S(1)} %get-tuple-element.28), channel_id=1, source_target_pairs={{1,0},{2,1},{3,2},{4,3},{5,4},{6,5},{7,6},{9,8},{10,9},{11,10},{12... | collective-permute-start | bytes 36872 | tf_op jit(solution)/shard_map/ppermute | solution.py:45
  204.3 23.1 %copy-start.4 = (f32[1,4096]{1,0:T(1,128)S(1)}, f32[1,4096]{1,0:T(1,128)}, u32[]{:S(2)}) copy-start(f32[1,4096]{1,0:T(1,128)} %param.13) | copy-start | bytes 49156
  204.3 23.1 %copy-start.1 = (f32[2,1,4096]{2,1,0:T(1,128)S(1)}, f32[2,1,4096]{2,1,0:T(1,128)}, u32[]{:S(2)}) copy-start(f32[2,1,4096]{2,1,0:T(1,128)} %param.14) | copy-start | bytes 98308
  204.3 23.1 %copy-start.2 = (f32[2,1,4096]{2,1,0:T(1,128)S(1)}, f32[2,1,4096]{2,1,0:T(1,128)}, u32[]{:S(2)}) copy-start(f32[2,1,4096]{2,1,0:T(1,128)} %param.15) | copy-start | bytes 98308
  338.3 21.1 %all-to-all-start.1 = ((bf16[2,128,1024]{1,0,2:T(2,128)(2,1)}), bf16[2,128,1024]{1,0,2:T(2,128)(2,1)S(1)}, u32[]{:S(2)}, u32[]{:S(2)}) async-start(bf16[2,128,1024]{1,0,2:T(2,128)(2,1)} %copy.18), calls=%async_computation.1 | async-start | bytes 1048576 | tf_op jit(solution)/shard_map/all_to_all | solution.py:159
Sparse Core Ops, SparseCore 0:
  79.3 21.3 reduce-scatter.1
where the time goes:
time: 407 us; the launch traced here: 400 us
  matrix products  198 us (49%)
  local copies, waits for them, and re-layouts  72.7 us (18%)
  other arithmetic  47.6 us (12%)
  waiting for transfers between devices  35.1 us (9%)
  starting transfers between devices  24.5 us (6%)
  between operations  15.4 us (4%)
  blocking collectives  6.54 us (2%)
    gather x1, local copies, waits for them, and re-layouts, data_part(): grid_real.reshape(-1)[places]  23 us
    gather x1, local copies, waits for them, and re-layouts, data_part(): grid_imag.reshape(-1)[places]  23 us
    scatter-add x1, other arithmetic, data_part(): hold_imag = jnp.zeros((cell_count,), jnp.float32).at[places].add(weighted...  22 us
    scatter-add x1, other arithmetic, data_part(): hold_real = jnp.zeros((cell_count,), jnp.float32).at[places].add(weighted...  22 us
    reduce_scatter x1, waiting for transfers between devices, wave_part(): lax.psum_scatter(squares.astype(jnp.bfloat16), 'chan', scatter_dimension=...  21.5 us
    dot_general x1, matrix products, data_part(): jnp.dot(flat_b, sin_table, preferred_element_type=jnp.float32)  17 us
    dot_general x1, matrix products, data_part(): lax.dot_general(returned[1], sin_table, leading, preferred_element_type=j...  16.9 us
    dot_general x1, matrix products, data_part(): jnp.dot(hold_imag, cos_table, preferred_element_type=jnp.float32)  16.5 us
  transfers between devices with their start and end apart: 7, of which 3 were waited for; matrix products, arithmetic and copies ran while one was open for 71% of the time, Pallas kernels for 0%

commit v1 on v0

--- a/solution.py
+++ b/solution.py
@@ -1,8 +1,12 @@
+import functools
 import math
 
 import jax
 import jax.numpy as jnp
+import numpy as np
 from jax import lax
+from jax.experimental import pallas as pl
+from jax.experimental.pallas import tpu as pltpu
 from jax.sharding import PartitionSpec as P
 
 N = 1024
@@ -188,7 +192,7 @@
     return (inner, fresh_dual)
 
 
-def local(image, margin, cells, weights, observed, dual_start):
+def local_plain(image, margin, cells, weights, observed, dual_start):
     count = image.shape[1]
     cos_table, sin_table = fourier_tables(N)
     row_map = row_matrix(count)
@@ -204,7 +208,330 @@
     return (fresh[None], dual[:, None, :])
 
 
+LANES = 128
+EDGE = 8
+CHUNK = 512
+highest = lax.Precision.HIGHEST
+crossed = (((1,), (1,)), ((), ()))
+
+
+def pick(offset, taps):
+    inside = (offset >= 0) & (offset < 8)
+    return np.where(inside, np.asarray(taps, np.float64)[np.clip(offset, 0, 7)], 0.0)
+
+
+def both_taps(offset, is_low):
+    return np.where(is_low, pick(offset, low_taps), pick(offset, high_taps)).astype(np.float32)
+
+
+def base_tables(length):
+    index = np.arange(length)[:, None] * np.arange(LANES)[None, :] % length
+    angle = index * (2.0 * np.pi / length)
+    scale = 1.0 / np.sqrt(length)
+    return np.stack([np.cos(angle) * scale, np.sin(angle) * scale]).astype(np.float32)
+
+
+def turn_tables(length):
+    blocks = length // LANES
+    turns = np.arange(blocks)[:, None] * np.arange(blocks)[None, :] % blocks
+    angle = turns * (2.0 * np.pi / blocks)
+    values = np.stack([np.cos(angle), np.sin(angle)])[..., None]
+    return np.broadcast_to(values, (2, blocks, blocks, LANES)).astype(np.float32)
+
+
+def analysis_map():
+    line = np.arange(4 * LANES)[:, None]
+    column = np.arange(2 * LANES)[None, :]
+    offset = line - (LANES - HALO) - 2 * (column % LANES)
+    return both_taps(offset, column < LANES)
+
+
+def synthesis_map():
+    line = np.arange(6 * LANES)[:, None]
+    column = np.arange(2 * LANES)[None, :]
+    block = line // (2 * LANES) - 1
+    offset = column - 2 * LANES * block - 2 * (line % LANES) + HALO
+    return both_taps(offset, line % (2 * LANES) < LANES)
+
+
+def wide_row_map(count):
+    half = count // 2
+    line = np.arange(count + 2 * EDGE)[:, None] - (EDGE - HALO)
+    column = np.arange(count)[None, :]
+    offset = line - 2 * (column % half)
+    return both_taps(offset, column < half)
+
+
+def whole_kernel(
+    n, c, img, margin, cells, gains, seen, dual, base, turn, m1, m2, rows, rows_t, out, vout,
+    tc, ts, hot, send1, recv1, send2, recv2, padded, halo, coef, sq, sq_in, cpad, spread, bands,
+    grid_hi, grid_lo, marks, hold,
+    sa, ra, sb, rb, sh, rh, ss, rs, sd, rd,
+):
+    me = lax.axis_index("slab")
+    ch = lax.axis_index("chan")
+    count, width = img.shape
+    blocks = width // LANES
+    vis = cells.shape[1]
+    after, before = lax.rem(me + 1, n), lax.rem(me + n - 1, n)
+
+    barrier = pltpu.get_barrier_semaphore()
+    for d in range(1, n):
+        pl.semaphore_signal(
+            barrier, inc=1, device_id={"slab": lax.rem(me + d, n)},
+            device_id_type=pl.DeviceIdType.MESH,
+        )
+    for d in range(1, c):
+        pl.semaphore_signal(
+            barrier, inc=1, device_id={"chan": lax.rem(ch + d, c)},
+            device_id_type=pl.DeviceIdType.MESH,
+        )
+
+    def remote(src, dst, s, r, where):
+        return pltpu.make_async_remote_copy(
+            src_ref=src, dst_ref=dst, send_sem=s, recv_sem=r, device_id=where,
+            device_id_type=pl.DeviceIdType.MESH,
+        )
+
+    base_c = base[0].reshape(width // 8, 8, LANES)
+    base_s = base[1].reshape(width // 8, 8, LANES)
+    for b in range(blocks):
+        kc, ks = turn[0, b][None], turn[1, b][None]
+        here = slice(b * LANES, (b + 1) * LANES)
+        tc[:, here] = (base_c * kc - base_s * ks).reshape(width, LANES).astype(jnp.bfloat16)
+        ts[:, here] = (base_s * kc + base_c * ks).reshape(width, LANES).astype(jnp.bfloat16)
+
+    flat_b = img[...].astype(jnp.bfloat16)
+    spec = lax.dot_general(tc[...], flat_b, crossed, preferred_element_type=jnp.float32)
+    send1[:, :count, :] = spec.astype(jnp.bfloat16).reshape(n, count, count)
+    spec = lax.dot_general(ts[...], flat_b, crossed, preferred_element_type=jnp.float32)
+    send1[:, count:, :] = (-spec).astype(jnp.bfloat16).reshape(n, count, count)
+
+    pl.semaphore_wait(barrier, n + c - 2)
+    up = remote(img.at[count - EDGE :], halo.at[0], sh.at[0], rh.at[0], {"slab": after})
+    down = remote(img.at[:EDGE], halo.at[1], sh.at[1], rh.at[1], {"slab": before})
+    up.start()
+    down.start()
+    sends1 = []
+    for d in range(1, n):
+        peer = lax.rem(me + d, n)
+        copy = remote(send1.at[peer], recv1.at[me], sa.at[d], ra.at[me], {"slab": peer})
+        copy.start()
+        sends1.append(copy)
+    recv1[me] = send1[me]
+
+    spot = cells[...]
+    low_spot = spot % width
+    step = 32
+
+    def make_hot(i, carry):
+        line = lax.broadcasted_iota(jnp.int32, (step, vis), 0) + i * step
+        hit = jnp.where(line == low_spot, 1.0, 0.0).astype(jnp.bfloat16)
+        hot[pl.ds(pl.multiple_of(i * step, step), step), :] = hit
+        return carry
+
+    lax.fori_loop(0, width // step, make_hot, 0)
+
+    reach = margin[0]
+    tall = count + 2 * EDGE
+
+    def keep(shape, dim):
+        line = lax.broadcasted_iota(jnp.int32, shape, dim)
+        distance = jnp.maximum(jnp.maximum(EDGE - line, line - count - EDGE + 1), 0)
+        return jnp.where(distance <= reach, 1.0, 0.0)
+
+    row_fwd = rows_t[...] * keep((count, tall), 1)
+    row_adj = rows[...] * keep((tall, count), 0)
+
+    padded[:, :LANES] = jnp.zeros((tall, LANES), jnp.float32)
+    padded[:, LANES + width :] = jnp.zeros((tall, LANES), jnp.float32)
+    padded[EDGE : EDGE + count, LANES : LANES + width] = img[...]
+    up.wait_recv()
+    down.wait_recv()
+    padded[:EDGE, LANES : LANES + width] = jnp.where(me > 0, halo[0], 0.0)
+    padded[EDGE + count :, LANES : LANES + width] = jnp.where(me < n - 1, halo[1], 0.0)
+    pair = 2 * LANES
+    for b in range(width // pair):
+        filtered = jnp.dot(
+            padded[:, b * pair : b * pair + 4 * LANES], m1[...], precision=highest,
+            preferred_element_type=jnp.float32,
+        )
+        part = jnp.dot(row_fwd, filtered, precision=highest, preferred_element_type=jnp.float32)
+        coef[:, b * pair : (b + 1) * pair] = part
+        sq[:, b * pair : (b + 1) * pair] = (part * part).astype(jnp.bfloat16)
+    sends_q = []
+    for d in range(1, c):
+        peer = lax.rem(ch + d, c)
+        copy = remote(sq, sq_in.at[ch], ss.at[d], rs.at[ch], {"chan": peer})
+        copy.start()
+        sends_q.append(copy)
+    sq_in[ch] = sq[...]
+
+    for d in range(1, n):
+        src = lax.rem(me + d, n)
+        remote(send1.at[src], recv1.at[src], sa.at[d], ra.at[src], {"slab": src}).wait_recv()
+    columns = jnp.concatenate([recv1[j] for j in range(n)], axis=1)
+    by_cos = jnp.dot(columns, tc[...], preferred_element_type=jnp.float32)
+    by_sin = jnp.dot(columns, ts[...], preferred_element_type=jnp.float32)
+    grid = jnp.concatenate(
+        [by_cos[:count] + by_sin[count:], by_cos[count:] - by_sin[:count]], axis=0
+    )
+    hi = grid.astype(jnp.bfloat16)
+    grid_hi[...] = hi
+    grid_lo[...] = (grid - hi.astype(jnp.float32)).astype(jnp.bfloat16)
+
+    def visit(i, carry):
+        here = pl.ds(pl.multiple_of(i * CHUNK, CHUNK), CHUNK)
+        table = hot[:, here]
+        found = jnp.dot(grid_hi[...], table, preferred_element_type=jnp.float32)
+        found = found + jnp.dot(grid_lo[...], table, preferred_element_type=jnp.float32)
+        line = lax.broadcasted_iota(jnp.int32, (count, CHUNK), 0)
+        match = line == cells[:, here] // width
+        gain = gains[:, here]
+        for part in range(2):
+            mine = found[part * count : (part + 1) * count]
+            value = jnp.sum(jnp.where(match, mine, 0.0), axis=0, keepdims=True)
+            fresh = (dual[part, :, here] + (gain * value - seen[part, :, here])) / 2.0
+            vout[part, :, here] = fresh
+            marks[part * count : (part + 1) * count, here] = jnp.where(
+                match, gain * fresh, 0.0
+            ).astype(jnp.bfloat16)
+        return carry
+
+    lax.fori_loop(0, vis // CHUNK, visit, 0)
+
+    def collect(i, carry):
+        here = pl.ds(pl.multiple_of(i * pair, pair), pair)
+        hold[here, :] = lax.dot_general(
+            hot[here, :], marks[...], crossed, preferred_element_type=jnp.float32
+        ).astype(jnp.bfloat16)
+        return carry
+
+    lax.fori_loop(0, width // pair, collect, 0)
+
+    sends2 = []
+    for d in range(1, n + 1):
+        peer = lax.rem(me + d, n)
+        here = pl.ds(pl.multiple_of(peer * count, count), count)
+        by_cos = jnp.dot(tc[here, :], hold[...], preferred_element_type=jnp.float32)
+        by_sin = jnp.dot(ts[here, :], hold[...], preferred_element_type=jnp.float32)
+        real = (by_cos[:, :count] - by_sin[:, count:]).astype(jnp.bfloat16)
+        imag = (by_sin[:, :count] + by_cos[:, count:]).astype(jnp.bfloat16)
+        if d < n:
+            send2[peer, :, :count] = real
+            send2[peer, :, count:] = imag
+            copy = remote(send2.at[peer], recv2.at[me], sb.at[d], rb.at[me], {"slab": peer})
+            copy.start()
+            sends2.append(copy)
+        else:
+            recv2[me, :, :count] = real
+            recv2[me, :, count:] = imag
+
+    for d in range(1, c):
+        src = lax.rem(ch + d, c)
+        remote(sq, sq_in.at[src], ss.at[d], rs.at[src], {"chan": src}).wait_recv()
+    cpad[:, :pair] = jnp.zeros((count, pair), jnp.float32)
+    cpad[:, pair + width :] = jnp.zeros((count, pair), jnp.float32)
+    for b in range(width // pair):
+        here = slice(b * pair, (b + 1) * pair)
+        total = sq_in[0, :, here].astype(jnp.float32)
+        for j in range(1, c):
+            total = total + sq_in[j, :, here].astype(jnp.float32)
+        factor = bound_level / jnp.maximum(jnp.sqrt(total), bound_level)
+        cpad[:, (b + 1) * pair : (b + 2) * pair] = coef[:, here] * factor
+    for b in range(width // pair):
+        back = jnp.dot(
+            cpad[:, b * pair : b * pair + 6 * LANES], m2[...], precision=highest,
+            preferred_element_type=jnp.float32,
+        )
+        spread[:, b * pair : (b + 1) * pair] = jnp.dot(
+            row_adj, back, precision=highest, preferred_element_type=jnp.float32
+        )
+    over = remote(spread.at[count + EDGE :], bands.at[0], sd.at[0], rd.at[0], {"slab": after})
+    under = remote(spread.at[:EDGE], bands.at[1], sd.at[1], rd.at[1], {"slab": before})
+    over.start()
+    under.start()
+    over.wait_recv()
+    under.wait_recv()
+    wave_first = spread[EDGE : 2 * EDGE, :] + jnp.where(me > 0, bands[0], 0.0)
+    wave_last = spread[count : count + EDGE, :] + jnp.where(me < n - 1, bands[1], 0.0)
+    wave = jnp.concatenate(
+        [wave_first, spread[2 * EDGE : count, :], wave_last], axis=0
+    )
+
+    for d in range(1, n):
+        src = lax.rem(me + d, n)
+        remote(send2.at[src], recv2.at[src], sb.at[d], rb.at[src], {"slab": src}).wait_recv()
+    real = jnp.concatenate([recv2[j, :, :count] for j in range(n)], axis=1)
+    imag = jnp.concatenate([recv2[j, :, count:] for j in range(n)], axis=1)
+    term = jnp.dot(real, tc[...], preferred_element_type=jnp.float32)
+    term = term - jnp.dot(imag, ts[...], preferred_element_type=jnp.float32)
+    out[...] = jnp.maximum(img[...] - tau_step * (term + wave), 0.0)
+
+    for copy in [up, down, over, under] + sends1 + sends_q + sends2:
+        copy.wait_send()
+
+
+def local_kernel(n, c, image, margin, cells, weights, observed, dual_start):
+    count, width = image.shape[1], image.shape[2]
+    vis = cells.shape[1]
+    tall = count + 2 * EDGE
+    half_t, f32 = jnp.bfloat16, jnp.float32
+    V = pltpu.VMEM
+    dma = pltpu.SemaphoreType.DMA
+    row_map = wide_row_map(count)
+    vm = pl.BlockSpec(memory_space=pltpu.VMEM)
+    fresh, dual = pl.pallas_call(
+        functools.partial(whole_kernel, n, c),
+        out_shape=(
+            jax.ShapeDtypeStruct((count, width), f32),
+            jax.ShapeDtypeStruct((2, 1, vis), f32),
+        ),
+        in_specs=[vm, pl.BlockSpec(memory_space=pltpu.SMEM)] + [vm] * 10,
+        out_specs=(vm, vm),
+        scratch_shapes=[
+            V((width, width), half_t),
+            V((width, width), half_t),
+            V((width, vis), half_t),
+            V((n, 2 * count, count), half_t),
+            V((n, 2 * count, count), half_t),
+            V((n, count, 2 * count), half_t),
+            V((n, count, 2 * count), half_t),
+            V((tall, width + 2 * LANES), f32),
+            V((2, EDGE, width), f32),
+            V((count, width), f32),
+            V((count, width), half_t),
+            V((c, count, width), half_t),
+            V((count, width + 4 * LANES), f32),
+            V((tall, width), f32),
+            V((2, EDGE, width), f32),
+            V((2 * count, width), half_t),
+            V((2 * count, width), half_t),
+            V((2 * count, vis), half_t),
+            V((width, 2 * count), half_t),
+            dma((n,)), dma((n,)), dma((n,)), dma((n,)), dma((2,)), dma((2,)),
+            dma((c,)), dma((c,)), dma((2,)), dma((2,)),
+        ],
+        compiler_params=pltpu.CompilerParams(
+            collective_id=0, has_side_effects=True, vmem_limit_bytes=60 * 1024 * 1024
+        ),
+    )(
+        image[0], margin, cells, weights, observed, dual_start,
+        base_tables(width), turn_tables(width), analysis_map(), synthesis_map(),
+        row_map, np.ascontiguousarray(row_map.T),
+    )
+    return (fresh[None], dual)
+
+
 def solution(mesh):
+    n, c = mesh.shape["slab"], mesh.shape["chan"]
+
+    def local(image, *rest):
+        count, width = image.shape[1], image.shape[2]
+        if count == LANES and width == 8 * LANES and rest[1].shape[1] % CHUNK == 0:
+            return local_kernel(n, c, image, *rest)
+        return local_plain(image, *rest)
+
     in_specs = (
         P("chan", "slab", None),
         P("slab"),

time: 407 us -> 49.9 us (0.12); the launches traced: 400 us -> 49.7 us
  matrix products: 198 us -> 0 us
  local copies, waits for them, and re-layouts: 72.7 us -> 2.51 us
  other arithmetic: 47.6 us -> 0 us
  Pallas kernels: 0 us -> 45.9 us
  waiting for transfers between devices: 35.1 us -> 0 us
  starting transfers between devices: 24.5 us -> 0 us
  between operations: 15.4 us -> 1.29 us
  blocking collectives: 6.54 us -> 0 us
    dot_general x14 -> x0, matrix products: 198 us -> none  [the longest x1 17 us: data_part(): jnp.dot(flat_b, sin_table, preferred_element_type=jnp.float32)]
    gather x2 -> x0, local copies, waits for them, and re-layouts: 46.1 us -> none  [the longest x1 23 us: data_part(): grid_real.reshape(-1)[places]]
    pallas_call x0 -> x1, Pallas kernels: none -> 45.9 us  [local_kernel(): pl.pallas_call(functools.partial(whole_kernel, n, c), out_shape=(jax.Shap...]
    scatter-add x2 -> x0, other arithmetic: 44.1 us -> none  [the longest x1 22 us: data_part(): hold_imag = jnp.zeros((cell_count,), jnp.float32).at[places].add(weighted...]
    slice x12 -> x0, local copies, waits for them, and re-layouts: 22.2 us -> none  [the longest x1 10.4 us: column_forward(): odd_cells = padded[:, 1::2]]
    reduce_scatter x1 -> x0, waiting for transfers between devices: 21.5 us -> none  [wave_part(): lax.psum_scatter(squares.astype(jnp.bfloat16), 'chan', scatter_dimension=...]
    all_to_all x2 -> x0, waiting for transfers between devices: 13.5 us -> none  [the longest x1 13.5 us: data_part(): lax.all_to_all(backward, 'slab', split_axis=2, concat_axis=1, tiled=True)]
    all_to_all x2 -> x0, starting transfers between devices: 12.9 us -> none  [the longest x1 6.64 us: data_part(): lax.all_to_all(backward, 'slab', split_axis=2, concat_axis=1, tiled=True)]
  transfers between devices with their start and end apart: 7 -> 0, of which waited for: 3 -> 0; matrix products, arithmetic and copies ran while one was open for 71% -> 0% of each run, Pallas kernels for 0% -> 0%
where the time goes in v1:
time: 49.9 us; the launch traced here: 49.7 us
  Pallas kernels  45.9 us (92%)
  local copies, waits for them, and re-layouts  2.51 us (5%)
  between operations  1.29 us (3%)
    pallas_call x1, Pallas kernels, local_kernel(): pl.pallas_call(functools.partial(whole_kernel, n, c), out_shape=(jax.Shap...  45.9 us
    unnamed x4, local copies, waits for them, and re-layouts  2.51 us

profile of v1, /device:TPU:0, one launch (start us, length us, event | category | flops | bytes accessed | tf_op | source)
XLA Modules:
  0.0 49.7 jit_solution(12584634315628454664)
XLA Ops:
  1.3 45.9 %shard_map.131 = (f32[128,1024]{1,0:T(8,128)}, f32[2,1,4096]{2,1,0:T(1,128)}) custom-call(f32[128,1024]{1,0:T(8,128)} %bitcast.3, s32[1]{0:T(128)S(6)} %copy.16.margin, s32[1,4096]{1,0:T(1,128)} %cells.1, f32[1,4096]{1,0:T(1,128)} %gains.1, f32[2,1,4096]{2,1,0:T(1,128)} %seen.1, f32[2,1,4096]{2,1,0:T(1,128)} %dual.1, f32[2,1024,128]{2,1,0:T(8,128)} %constant.12.clone.base, ...), custom_call_target="tpu_custom_call" | custom-call | tf_op jit(solution)/shard_map/pallas_call | solution.py:484
  47.2 0.0 copy-start
  47.2 1.9 %copy.17 = f32[1,128,1024]{2,1,0:T(8,128)} copy(f32[1,128,1024]{2,1,0:T(8,128)} %bitcast.2) | data formatting | bytes 1048576
  49.1 0.0 copy-done
  49.1 0.6 %copy.18 = f32[2,1,4096]{2,1,0:T(1,128)} copy(f32[2,1,4096]{2,1,0:T(1,128)S(1)} %copy-done) | data formatting | bytes 65536
Async XLA Ops:
  47.2 1.9 %copy-start = (f32[2,1,4096]{2,1,0:T(1,128)S(1)}, f32[2,1,4096]{2,1,0:T(1,128)}, u32[]{:S(2)}) copy-start(f32[2,1,4096]{2,1,0:T(1,128)} %get-tuple-element.9) | copy-start | bytes 98308

commit v2 on v1

--- a/solution.py
+++ b/solution.py
@@ -262,10 +262,35 @@
     return both_taps(offset, column < half)
 
 
+def in_two(values):
+    top = values.astype(jnp.bfloat16)
+    return np.stack([top, (values - top.astype(np.float32)).astype(jnp.bfloat16)])
+
+
+def split(value):
+    top = value.astype(jnp.bfloat16)
+    return top, (value - top.astype(jnp.float32)).astype(jnp.bfloat16)
+
+
+def fine_dot(left, right):
+    total = jnp.dot(left[0], right[0], preferred_element_type=jnp.float32)
+    total = total + jnp.dot(left[1], right[0], preferred_element_type=jnp.float32)
+    return total + jnp.dot(left[0], right[1], preferred_element_type=jnp.float32)
+
+
+def flip(place, bits):
+    result = place
+    for bit in (1, 2, 4):
+        if bits & bit:
+            result = result + bit - 2 * bit * (place // bit % 2)
+    return result
+
+
 def whole_kernel(
-    n, c, img, margin, cells, gains, seen, dual, base, turn, m1, m2, rows, rows_t, out, vout,
+    n, c, img, margin, cells, gains, seen, dual, base, turn, m1_far, m2_far, rows_far, rows_t_far,
+    out, vout, m1, m2, rows, rows_t, fetched, found_half,
     tc, ts, hot, send1, recv1, send2, recv2, padded, halo, coef, sq, sq_in, cpad, spread, bands,
-    grid_hi, grid_lo, marks, hold,
+    grid, marks, hold, u_spot,
     sa, ra, sb, rb, sh, rh, ss, rs, sd, rd,
 ):
     me = lax.axis_index("slab")
@@ -293,6 +318,15 @@
             device_id_type=pl.DeviceIdType.MESH,
         )
 
+    fetches = [
+        pltpu.make_async_copy(far, near, fetched.at[i])
+        for i, (far, near) in enumerate(
+            [(m1_far, m1), (rows_far, rows), (rows_t_far, rows_t), (m2_far, m2)]
+        )
+    ]
+    for fetch in fetches:
+        fetch.start()
+
     base_c = base[0].reshape(width // 8, 8, LANES)
     base_s = base[1].reshape(width // 8, 8, LANES)
     for b in range(blocks):
@@ -302,10 +336,11 @@
         ts[:, here] = (base_s * kc + base_c * ks).reshape(width, LANES).astype(jnp.bfloat16)
 
     flat_b = img[...].astype(jnp.bfloat16)
+    part = count // 2
     spec = lax.dot_general(tc[...], flat_b, crossed, preferred_element_type=jnp.float32)
-    send1[:, :count, :] = spec.astype(jnp.bfloat16).reshape(n, count, count)
+    send1[:, :, :part, :] = spec.astype(jnp.bfloat16).reshape(n, 2, part, count)
     spec = lax.dot_general(ts[...], flat_b, crossed, preferred_element_type=jnp.float32)
-    send1[:, count:, :] = (-spec).astype(jnp.bfloat16).reshape(n, count, count)
+    send1[:, :, part:, :] = (-spec).astype(jnp.bfloat16).reshape(n, 2, part, count)
 
     pl.semaphore_wait(barrier, n + c - 2)
     up = remote(img.at[count - EDGE :], halo.at[0], sh.at[0], rh.at[0], {"slab": after})
@@ -313,11 +348,14 @@
     up.start()
     down.start()
     sends1 = []
-    for d in range(1, n):
-        peer = lax.rem(me + d, n)
-        copy = remote(send1.at[peer], recv1.at[me], sa.at[d], ra.at[me], {"slab": peer})
-        copy.start()
-        sends1.append(copy)
+    for h in range(2):
+        for d in range(n - 1, 0, -1):
+            peer = flip(me, d)
+            copy = remote(
+                send1.at[peer, h], recv1.at[me, h], sa.at[h, d], ra.at[h, me], {"slab": peer}
+            )
+            copy.start()
+            sends1.append(copy)
     recv1[me] = send1[me]
 
     spot = cells[...]
@@ -340,8 +378,10 @@
         distance = jnp.maximum(jnp.maximum(EDGE - line, line - count - EDGE + 1), 0)
         return jnp.where(distance <= reach, 1.0, 0.0)
 
-    row_fwd = rows_t[...] * keep((count, tall), 1)
-    row_adj = rows[...] * keep((tall, count), 0)
+    for fetch in fetches:
+        fetch.wait()
+    row_fwd = split(rows_t[...] * keep((count, tall), 1))
+    row_adj = split(rows[...] * keep((tall, count), 0))
 
     padded[:, :LANES] = jnp.zeros((tall, LANES), jnp.float32)
     padded[:, LANES + width :] = jnp.zeros((tall, LANES), jnp.float32)
@@ -352,13 +392,10 @@
     padded[EDGE + count :, LANES : LANES + width] = jnp.where(me < n - 1, halo[1], 0.0)
     pair = 2 * LANES
     for b in range(width // pair):
-        filtered = jnp.dot(
-            padded[:, b * pair : b * pair + 4 * LANES], m1[...], precision=highest,
-            preferred_element_type=jnp.float32,
-        )
-        part = jnp.dot(row_fwd, filtered, precision=highest, preferred_element_type=jnp.float32)
-        coef[:, b * pair : (b + 1) * pair] = part
-        sq[:, b * pair : (b + 1) * pair] = (part * part).astype(jnp.bfloat16)
+        filtered = fine_dot(split(padded[:, b * pair : b * pair + 4 * LANES]), m1)
+        piece = fine_dot(row_fwd, split(filtered))
+        coef[:, b * pair : (b + 1) * pair] = piece
+        sq[:, b * pair : (b + 1) * pair] = (piece * piece).astype(jnp.bfloat16)
     sends_q = []
     for d in range(1, c):
         peer = lax.rem(ch + d, c)
@@ -367,57 +404,70 @@
         sends_q.append(copy)
     sq_in[ch] = sq[...]
 
-    for d in range(1, n):
-        src = lax.rem(me + d, n)
-        remote(send1.at[src], recv1.at[src], sa.at[d], ra.at[src], {"slab": src}).wait_recv()
-    columns = jnp.concatenate([recv1[j] for j in range(n)], axis=1)
-    by_cos = jnp.dot(columns, tc[...], preferred_element_type=jnp.float32)
-    by_sin = jnp.dot(columns, ts[...], preferred_element_type=jnp.float32)
-    grid = jnp.concatenate(
-        [by_cos[:count] + by_sin[count:], by_cos[count:] - by_sin[:count]], axis=0
-    )
-    hi = grid.astype(jnp.bfloat16)
-    grid_hi[...] = hi
-    grid_lo[...] = (grid - hi.astype(jnp.float32)).astype(jnp.bfloat16)
-
-    def visit(i, carry):
+    u_spot[...] = spot // width
+
+    def look(h, here):
+        found = jnp.dot(grid[h], hot[:, here], preferred_element_type=jnp.float32)
+        found = found[:count] + found[count:]
+        line = lax.broadcasted_iota(jnp.int32, (part, CHUNK), 0) + h * part
+        match = line == u_spot[:, here]
+        return [
+            jnp.sum(
+                jnp.where(match, found[k * part : (k + 1) * part], 0.0), axis=0, keepdims=True
+            )
+            for k in range(2)
+        ]
+
+    def visit_first(i, carry):
         here = pl.ds(pl.multiple_of(i * CHUNK, CHUNK), CHUNK)
-        table = hot[:, here]
-        found = jnp.dot(grid_hi[...], table, preferred_element_type=jnp.float32)
-        found = found + jnp.dot(grid_lo[...], table, preferred_element_type=jnp.float32)
+        values = look(0, here)
+        for k in range(2):
+            found_half[k, :, here] = values[k]
+        return carry
+
+    def visit_last(i, carry):
+        here = pl.ds(pl.multiple_of(i * CHUNK, CHUNK), CHUNK)
+        values = look(1, here)
         line = lax.broadcasted_iota(jnp.int32, (count, CHUNK), 0)
-        match = line == cells[:, here] // width
+        match = line == u_spot[:, here]
         gain = gains[:, here]
-        for part in range(2):
-            mine = found[part * count : (part + 1) * count]
-            value = jnp.sum(jnp.where(match, mine, 0.0), axis=0, keepdims=True)
-            fresh = (dual[part, :, here] + (gain * value - seen[part, :, here])) / 2.0
-            vout[part, :, here] = fresh
-            marks[part * count : (part + 1) * count, here] = jnp.where(
+        for k in range(2):
+            value = values[k] + found_half[k, :, here]
+            fresh = (dual[k, :, here] + (gain * value - seen[k, :, here])) / 2.0
+            vout[k, :, here] = fresh
+            marks[k * count : (k + 1) * count, here] = jnp.where(
                 match, gain * fresh, 0.0
             ).astype(jnp.bfloat16)
         return carry
 
-    lax.fori_loop(0, vis // CHUNK, visit, 0)
-
-    def collect(i, carry):
-        here = pl.ds(pl.multiple_of(i * pair, pair), pair)
-        hold[here, :] = lax.dot_general(
-            hot[here, :], marks[...], crossed, preferred_element_type=jnp.float32
-        ).astype(jnp.bfloat16)
-        return carry
-
-    lax.fori_loop(0, width // pair, collect, 0)
+    for h in range(2):
+        for d in range(n - 1, 0, -1):
+            src = flip(me, d)
+            remote(
+                send1.at[src, h], recv1.at[src, h], sa.at[h, d], ra.at[h, src], {"slab": src}
+            ).wait_recv()
+        columns = jnp.concatenate([recv1[j, h] for j in range(n)], axis=1)
+        by_cos = jnp.dot(columns, tc[...], preferred_element_type=jnp.float32)
+        by_sin = jnp.dot(columns, ts[...], preferred_element_type=jnp.float32)
+        values = jnp.concatenate(
+            [by_cos[:part] + by_sin[part:], by_cos[part:] - by_sin[:part]], axis=0
+        )
+        grid[h] = jnp.concatenate(split(values), axis=0)
+        lax.fori_loop(0, vis // CHUNK, (visit_first, visit_last)[h], 0, unroll=2)
+
+    hold[...] = lax.dot_general(
+        hot[...], marks[...], crossed, preferred_element_type=jnp.float32
+    ).astype(jnp.bfloat16)
 
     sends2 = []
-    for d in range(1, n + 1):
-        peer = lax.rem(me + d, n)
+    for d in range(n - 1, -1, -1):
+        peer = flip(me, d)
         here = pl.ds(pl.multiple_of(peer * count, count), count)
         by_cos = jnp.dot(tc[here, :], hold[...], preferred_element_type=jnp.float32)
         by_sin = jnp.dot(ts[here, :], hold[...], preferred_element_type=jnp.float32)
         real = (by_cos[:, :count] - by_sin[:, count:]).astype(jnp.bfloat16)
         imag = (by_sin[:, :count] + by_cos[:, count:]).astype(jnp.bfloat16)
-        if d < n:
+        if d > 0:
             send2[peer, :, :count] = real
             send2[peer, :, count:] = imag
             copy = remote(send2.at[peer], recv2.at[me], sb.at[d], rb.at[me], {"slab": peer})
@@ -440,17 +490,28 @@
         factor = bound_level / jnp.maximum(jnp.sqrt(total), bound_level)
         cpad[:, (b + 1) * pair : (b + 2) * pair] = coef[:, here] * factor
     for b in range(width // pair):
-        back = jnp.dot(
-            cpad[:, b * pair : b * pair + 6 * LANES], m2[...], precision=highest,
-            preferred_element_type=jnp.float32,
-        )
-        spread[:, b * pair : (b + 1) * pair] = jnp.dot(
-            row_adj, back, precision=highest, preferred_element_type=jnp.float32
-        )
+        back = fine_dot(split(cpad[:, b * pair : b * pair + 6 * LANES]), m2)
+        spread[:, b * pair : (b + 1) * pair] = fine_dot(row_adj, split(back))
     over = remote(spread.at[count + EDGE :], bands.at[0], sd.at[0], rd.at[0], {"slab": after})
     under = remote(spread.at[:EDGE], bands.at[1], sd.at[1], rd.at[1], {"slab": before})
     over.start()
     under.start()
+
+    side = n // 2
+    term = None
+    for far in range(2):
+        for d in range(1 - far, side):
+            src = flip(me, d + far * side)
+            remote(
+                send2.at[src], recv2.at[src], sb.at[d + far * side], rb.at[src], {"slab": src}
+            ).wait_recv()
+        first = (me // side + far) % 2 * side
+        real = jnp.concatenate([recv2[first + j, :, :count] for j in range(side)], axis=1)
+        imag = jnp.concatenate([recv2[first + j, :, count:] for j in range(side)], axis=1)
+        here = pl.ds(pl.multiple_of(first * count, count), side * count)
+        more = jnp.dot(real, tc[here, :], preferred_element_type=jnp.float32)
+        more = more - jnp.dot(imag, ts[here, :], preferred_element_type=jnp.float32)
+        term = more if term is None else term + more
     over.wait_recv()
     under.wait_recv()
     wave_first = spread[EDGE : 2 * EDGE, :] + jnp.where(me > 0, bands[0], 0.0)
@@ -458,14 +519,6 @@
     wave = jnp.concatenate(
         [wave_first, spread[2 * EDGE : count, :], wave_last], axis=0
     )
-
-    for d in range(1, n):
-        src = lax.rem(me + d, n)
-        remote(send2.at[src], recv2.at[src], sb.at[d], rb.at[src], {"slab": src}).wait_recv()
-    real = jnp.concatenate([recv2[j, :, :count] for j in range(n)], axis=1)
-    imag = jnp.concatenate([recv2[j, :, count:] for j in range(n)], axis=1)
-    term = jnp.dot(real, tc[...], preferred_element_type=jnp.float32)
-    term = term - jnp.dot(imag, ts[...], preferred_element_type=jnp.float32)
     out[...] = jnp.maximum(img[...] - tau_step * (term + wave), 0.0)
 
     for copy in [up, down, over, under] + sends1 + sends_q + sends2:
@@ -487,14 +540,21 @@
             jax.ShapeDtypeStruct((count, width), f32),
             jax.ShapeDtypeStruct((2, 1, vis), f32),
         ),
-        in_specs=[vm, pl.BlockSpec(memory_space=pltpu.SMEM)] + [vm] * 10,
+        in_specs=[vm, pl.BlockSpec(memory_space=pltpu.SMEM)] + [vm] * 6
+        + [pl.BlockSpec(memory_space=pl.ANY)] * 4,
         out_specs=(vm, vm),
         scratch_shapes=[
+            V((2, 4 * LANES, 2 * LANES), half_t),
+            V((2, 6 * LANES, 2 * LANES), half_t),
+            V((tall, count), f32),
+            V((count, tall), f32),
+            dma((4,)),
+            V((2, 1, vis), f32),
             V((width, width), half_t),
             V((width, width), half_t),
             V((width, vis), half_t),
-            V((n, 2 * count, count), half_t),
-            V((n, 2 * count, count), half_t),
+            V((n, 2, count, count), half_t),
+            V((n, 2, count, count), half_t),
             V((n, count, 2 * count), half_t),
             V((n, count, 2 * count), half_t),
             V((tall, width + 2 * LANES), f32),
@@ -505,19 +565,19 @@
             V((count, width + 4 * LANES), f32),
             V((tall, width), f32),
             V((2, EDGE, width), f32),
-            V((2 * count, width), half_t),
-            V((2 * count, width), half_t),
+            V((2, 2 * count, width), half_t),
             V((2 * count, vis), half_t),
             V((width, 2 * count), half_t),
-            dma((n,)), dma((n,)), dma((n,)), dma((n,)), dma((2,)), dma((2,)),
+            V((1, vis), jnp.int32),
+            dma((2, n)), dma((2, n)), dma((n,)), dma((n,)), dma((2,)), dma((2,)),
             dma((c,)), dma((c,)), dma((2,)), dma((2,)),
         ],
         compiler_params=pltpu.CompilerParams(
-            collective_id=0, has_side_effects=True, vmem_limit_bytes=60 * 1024 * 1024
+            collective_id=0, has_side_effects=True, vmem_limit_bytes=40 * 1024 * 1024
         ),
     )(
         image[0], margin, cells, weights, observed, dual_start,
-        base_tables(width), turn_tables(width), analysis_map(), synthesis_map(),
+        base_tables(width), turn_tables(width), in_two(analysis_map()), in_two(synthesis_map()),
         row_map, np.ascontiguousarray(row_map.T),
     )
     return (fresh[None], dual)
@@ -528,7 +588,7 @@
 
     def local(image, *rest):
         count, width = image.shape[1], image.shape[2]
-        if count == LANES and width == 8 * LANES and rest[1].shape[1] % CHUNK == 0:
+        if n == 8 and count == LANES and width == n * count and rest[1].shape[1] % CHUNK == 0:
             return local_kernel(n, c, image, *rest)
         return local_plain(image, *rest)
 

time: 49.9 us -> 54.3 us (1.088)
  local copies, waits for them, and re-layouts: 2.51 us -> 11.4 us
  Pallas kernels: 45.9 us -> 40.9 us
    unnamed x4 -> x24, local copies, waits for them, and re-layouts: 2.51 us -> 11.4 us
    pallas_call x1, Pallas kernels: 45.9 us -> 40.9 us  [local_kernel(): pl.pallas_call(functools.partial(whole_kernel, n, c), out_shape=(jax.Shap...]
where the time goes in v2:
time: 54.3 us; the launch traced here: 53.6 us
  Pallas kernels  40.9 us (75%)
  local copies, waits for them, and re-layouts  11.4 us (21%)
  between operations  1.3 us (2%)
    pallas_call x1, Pallas kernels, local_kernel(): pl.pallas_call(functools.partial(whole_kernel, n, c), out_shape=(jax.Shap...  40.9 us
    unnamed x24, local copies, waits for them, and re-layouts  11.4 us

profile of v2, /device:TPU:0, one launch (start us, length us, event | category | flops | bytes accessed | tf_op | source)
XLA Modules:
  0.0 53.6 jit_solution(3540142574906078942)
XLA Ops:
  1.3 0.0 copy-start
  1.3 1.2 %copy-done = f32[2,1024,128]{2,1,0:T(8,128)S(1)} copy-done((f32[2,1024,128]{2,1,0:T(8,128)S(1)}, f32[2,1024,128]{2,1,0:T(8,128)}, u32[]{:S(2)}) %copy-start) | copy-done | bytes 1048600
  2.5 0.0 copy-start.1
  2.5 1.1 %copy-done.1 = bf16[2,768,256]{2,1,0:T(8,128)(2,1)S(1)} copy-done((bf16[2,768,256]{2,1,0:T(8,128)(2,1)S(1)}, bf16[2,768,256]{2,1,0:T(8,128)(2,1)}, u32[]{:S(2)}) %copy-start.1) | copy-done | bytes 786456
  3.6 0.0 copy-start.2
  3.6 1.0 %copy-done.2 = f32[1,128,1024]{2,1,0:T(8,128)S(1)} copy-done((f32[1,128,1024]{2,1,0:T(8,128)S(1)}, f32[1,128,1024]{2,1,0:T(8,128)}, u32[]{:S(2)}) %copy-start.2) | copy-done | bytes 524312
  4.7 0.0 copy-start.3
  4.7 1.0 %copy-done.3 = bf16[2,512,256]{2,1,0:T(8,128)(2,1)S(1)} copy-done((bf16[2,512,256]{2,1,0:T(8,128)(2,1)S(1)}, bf16[2,512,256]{2,1,0:T(8,128)(2,1)}, u32[]{:S(2)}) %copy-start.3) | copy-done | bytes 524312
  5.7 0.0 copy-start.4
  5.7 0.9 %copy-done.4 = f32[128,144]{1,0:T(8,128)S(1)} copy-done((f32[128,144]{1,0:T(8,128)S(1)}, f32[128,144]{1,0:T(8,128)}, u32[]{:S(2)}) %copy-start.4) | copy-done | bytes 73752
  6.6 0.0 copy-start.5
  6.6 0.9 %copy-done.5 = f32[144,128]{1,0:T(8,128)S(1)} copy-done((f32[144,128]{1,0:T(8,128)S(1)}, f32[144,128]{1,0:T(8,128)}, u32[]{:S(2)}) %copy-start.5) | copy-done | bytes 73752
  7.5 0.0 copy-start.6
  7.5 0.8 %copy-done.6 = f32[2,8,8,128]{3,2,1,0:T(8,128)S(1)} copy-done((f32[2,8,8,128]{3,2,1,0:T(8,128)S(1)}, f32[2,8,8,128]{3,2,1,0:T(8,128)}, u32[]{:S(2)}) %copy-start.6) | copy-done | bytes 65560
  8.4 0.0 copy-start.7
  8.4 0.8 %copy-done.7 = f32[2,1,4096]{2,1,0:T(1,128)S(1)} copy-done((f32[2,1,4096]{2,1,0:T(1,128)S(1)}, f32[2,1,4096]{2,1,0:T(1,128)}, u32[]{:S(2)}) %copy-start.7) | copy-done | bytes 32792
  9.1 0.0 copy-start.8
  9.1 0.8 %copy-done.8 = f32[2,1,4096]{2,1,0:T(1,128)S(1)} copy-done((f32[2,1,4096]{2,1,0:T(1,128)S(1)}, f32[2,1,4096]{2,1,0:T(1,128)}, u32[]{:S(2)}) %copy-start.8) | copy-done | bytes 32792
  9.9 0.0 copy-start.9
  9.9 0.7 %copy-done.9 = s32[1,4096]{1,0:T(1,128)S(1)} copy-done((s32[1,4096]{1,0:T(1,128)S(1)}, s32[1,4096]{1,0:T(1,128)}, u32[]{:S(2)}) %copy-start.9) | copy-done | bytes 16408
  10.6 0.0 copy-start.10
  10.6 0.7 %copy-done.10 = f32[1,4096]{1,0:T(1,128)S(1)} copy-done((f32[1,4096]{1,0:T(1,128)S(1)}, f32[1,4096]{1,0:T(1,128)}, u32[]{:S(2)}) %copy-start.10) | copy-done | bytes 16408
  11.3 40.9 %shard_map.131 = (f32[128,1024]{1,0:T(8,128)S(1)}, f32[2,1,4096]{2,1,0:T(1,128)S(1)}) custom-call(f32[128,1024]{1,0:T(8,128)S(1)} %bitcast.3, s32[1]{0:T(128)S(6)} %copy.16.margin, s32[1,4096]{1,0:T(1,128)S(1)} %copy-done.9, f32[1,4096]{1,0:T(1,128)S(1)} %copy-done.10, f32[2,1,4096]{2,1,0:T(1,128)S(1)} %copy-done.7, f32[2,1,4096]{2,1,0:T(1,128)S(1)} %copy-done.8, ...), custom_call_target="tpu_custom_call" | custom-call | tf_op jit(solution)/shard_map/pallas_call | solution.py:537
  52.2 0.8 %copy.17 = f32[1,128,1024]{2,1,0:T(8,128)} copy(f32[1,128,1024]{2,1,0:T(8,128)S(1)} %bitcast.2) | data formatting | bytes 1048576
  53.0 0.6 %copy.18 = f32[2,1,4096]{2,1,0:T(1,128)} copy(f32[2,1,4096]{2,1,0:T(1,128)S(1)} %get-tuple-element.9) | data formatting | bytes 65536
Async XLA Ops:
  1.3 1.2 %copy-start = (f32[2,1024,128]{2,1,0:T(8,128)S(1)}, f32[2,1024,128]{2,1,0:T(8,128)}, u32[]{:S(2)}) copy-start(f32[2,1024,128]{2,1,0:T(8,128)} %constant.12.clone.base) | copy-start | bytes 3145732
  2.5 1.1 %copy-start.1 = (bf16[2,768,256]{2,1,0:T(8,128)(2,1)S(1)}, bf16[2,768,256]{2,1,0:T(8,128)(2,1)}, u32[]{:S(2)}) copy-start(bf16[2,768,256]{2,1,0:T(8,128)(2,1)} %constant.15.clone.m2_far) | copy-start | bytes 2359300
  3.6 1.0 %copy-start.2 = (f32[1,128,1024]{2,1,0:T(8,128)S(1)}, f32[1,128,1024]{2,1,0:T(8,128)}, u32[]{:S(2)}) copy-start(f32[1,128,1024]{2,1,0:T(8,128)} %param.12) | copy-start | bytes 1572868
  4.7 1.0 %copy-start.3 = (bf16[2,512,256]{2,1,0:T(8,128)(2,1)S(1)}, bf16[2,512,256]{2,1,0:T(8,128)(2,1)}, u32[]{:S(2)}) copy-start(bf16[2,512,256]{2,1,0:T(8,128)(2,1)} %constant.14.clone.m1_far) | copy-start | bytes 1572868
  5.7 0.9 %copy-start.4 = (f32[128,144]{1,0:T(8,128)S(1)}, f32[128,144]{1,0:T(8,128)}, u32[]{:S(2)}) copy-start(f32[128,144]{1,0:T(8,128)} %constant.17.clone.rows_t_far) | copy-start | bytes 221188
  6.6 0.9 %copy-start.5 = (f32[144,128]{1,0:T(8,128)S(1)}, f32[144,128]{1,0:T(8,128)}, u32[]{:S(2)}) copy-start(f32[144,128]{1,0:T(8,128)} %constant.16.clone.rows_far) | copy-start | bytes 221188
  7.5 0.8 %copy-start.6 = (f32[2,8,8,128]{3,2,1,0:T(8,128)S(1)}, f32[2,8,8,128]{3,2,1,0:T(8,128)}, u32[]{:S(2)}) copy-start(f32[2,8,8,128]{3,2,1,0:T(8,128)} %constant.13.clone.turn) | copy-start | bytes 196612
  8.4 0.8 %copy-start.7 = (f32[2,1,4096]{2,1,0:T(1,128)S(1)}, f32[2,1,4096]{2,1,0:T(1,128)}, u32[]{:S(2)}) copy-start(f32[2,1,4096]{2,1,0:T(1,128)} %seen.1) | copy-start | bytes 98308
  9.1 0.8 %copy-start.8 = (f32[2,1,4096]{2,1,0:T(1,128)S(1)}, f32[2,1,4096]{2,1,0:T(1,128)}, u32[]{:S(2)}) copy-start(f32[2,1,4096]{2,1,0:T(1,128)} %dual.1) | copy-start | bytes 98308
  9.9 0.7 %copy-start.9 = (s32[1,4096]{1,0:T(1,128)S(1)}, s32[1,4096]{1,0:T(1,128)}, u32[]{:S(2)}) copy-start(s32[1,4096]{1,0:T(1,128)} %cells.1) | copy-start | bytes 49156
  10.6 0.7 %copy-start.10 = (f32[1,4096]{1,0:T(1,128)S(1)}, f32[1,4096]{1,0:T(1,128)}, u32[]{:S(2)}) copy-start(f32[1,4096]{1,0:T(1,128)} %gains.1) | copy-start | bytes 49156

commit v3 on v2

--- a/solution.py
+++ b/solution.py
@@ -287,8 +287,10 @@
 
 
 def whole_kernel(
-    n, c, img, margin, cells, gains, seen, dual, base, turn, m1_far, m2_far, rows_far, rows_t_far,
-    out, vout, m1, m2, rows, rows_t, fetched, found_half,
+    n, c, img_far, margin_far, cells_far, gains_far, seen_far, dual_far, base_far, turn_far, m1_far,
+    m2_far, rows_far, rows_t_far,
+    out, vout, img, margin, cells, gains, seen, dual, base, turn, m1, m2, rows, rows_t, fetched,
+    found_half,
     tc, ts, hot, send1, recv1, send2, recv2, padded, halo, coef, sq, sq_in, cpad, spread, bands,
     grid, marks, hold, u_spot,
     sa, ra, sb, rb, sh, rh, ss, rs, sd, rd,
@@ -299,6 +301,19 @@
     blocks = width // LANES
     vis = cells.shape[1]
     after, before = lax.rem(me + 1, n), lax.rem(me + n - 1, n)
+
+    fetches = [
+        pltpu.make_async_copy(far, near, fetched.at[i])
+        for i, (far, near) in enumerate(
+            [
+                (base_far, base), (turn_far, turn), (img_far, img), (cells_far, cells),
+                (m1_far, m1), (rows_t_far, rows_t), (margin_far, margin), (rows_far, rows),
+                (gains_far, gains), (seen_far, seen), (dual_far, dual), (m2_far, m2),
+            ]
+        )
+    ]
+    for fetch in fetches:
+        fetch.start()
 
     barrier = pltpu.get_barrier_semaphore()
     for d in range(1, n):
@@ -318,15 +333,8 @@
             device_id_type=pl.DeviceIdType.MESH,
         )
 
-    fetches = [
-        pltpu.make_async_copy(far, near, fetched.at[i])
-        for i, (far, near) in enumerate(
-            [(m1_far, m1), (rows_far, rows), (rows_t_far, rows_t), (m2_far, m2)]
-        )
-    ]
-    for fetch in fetches:
-        fetch.start()
-
+    for fetch in fetches[:2]:
+        fetch.wait()
     base_c = base[0].reshape(width // 8, 8, LANES)
     base_s = base[1].reshape(width // 8, 8, LANES)
     for b in range(blocks):
@@ -335,6 +343,7 @@
         tc[:, here] = (base_c * kc - base_s * ks).reshape(width, LANES).astype(jnp.bfloat16)
         ts[:, here] = (base_s * kc + base_c * ks).reshape(width, LANES).astype(jnp.bfloat16)
 
+    fetches[2].wait()
     flat_b = img[...].astype(jnp.bfloat16)
     part = count // 2
     spec = lax.dot_general(tc[...], flat_b, crossed, preferred_element_type=jnp.float32)
@@ -358,6 +367,7 @@
             sends1.append(copy)
     recv1[me] = send1[me]
 
+    fetches[3].wait()
     spot = cells[...]
     low_spot = spot % width
     step = 32
@@ -370,7 +380,6 @@
 
     lax.fori_loop(0, width // step, make_hot, 0)
 
-    reach = margin[0]
     tall = count + 2 * EDGE
 
     def keep(shape, dim):
@@ -378,8 +387,9 @@
         distance = jnp.maximum(jnp.maximum(EDGE - line, line - count - EDGE + 1), 0)
         return jnp.where(distance <= reach, 1.0, 0.0)
 
-    for fetch in fetches:
+    for fetch in fetches[4:]:
         fetch.wait()
+    reach = margin[0]
     row_fwd = split(rows_t[...] * keep((count, tall), 1))
     row_adj = split(rows[...] * keep((tall, count), 0))
 
@@ -455,9 +465,14 @@
         grid[h] = jnp.concatenate(split(values), axis=0)
         lax.fori_loop(0, vis // CHUNK, (visit_first, visit_last)[h], 0, unroll=2)
 
-    hold[...] = lax.dot_general(
-        hot[...], marks[...], crossed, preferred_element_type=jnp.float32
-    ).astype(jnp.bfloat16)
+    def collect(i, carry):
+        here = pl.ds(pl.multiple_of(i * pair, pair), pair)
+        hold[here, :] = lax.dot_general(
+            hot[here, :], marks[...], crossed, preferred_element_type=jnp.float32
+        ).astype(jnp.bfloat16)
+        return carry
+
+    lax.fori_loop(0, width // pair, collect, 0)
 
     sends2 = []
     for d in range(n - 1, -1, -1):
@@ -540,15 +555,22 @@
             jax.ShapeDtypeStruct((count, width), f32),
             jax.ShapeDtypeStruct((2, 1, vis), f32),
         ),
-        in_specs=[vm, pl.BlockSpec(memory_space=pltpu.SMEM)] + [vm] * 6
-        + [pl.BlockSpec(memory_space=pl.ANY)] * 4,
+        in_specs=[pl.BlockSpec(memory_space=pl.ANY)] * 12,
         out_specs=(vm, vm),
         scratch_shapes=[
+            V((count, width), f32),
+            pltpu.SMEM((1,), jnp.int32),
+            V((1, vis), jnp.int32),
+            V((1, vis), f32),
+            V((2, 1, vis), f32),
+            V((2, 1, vis), f32),
+            V((2, width, LANES), f32),
+            V((2, n, n, LANES), f32),
             V((2, 4 * LANES, 2 * LANES), half_t),
             V((2, 6 * LANES, 2 * LANES), half_t),
             V((tall, count), f32),
             V((count, tall), f32),
-            dma((4,)),
+            dma((12,)),
             V((2, 1, vis), f32),
             V((width, width), half_t),
             V((width, width), half_t),
@@ -573,7 +595,7 @@
             dma((c,)), dma((c,)), dma((2,)), dma((2,)),
         ],
         compiler_params=pltpu.CompilerParams(
-            collective_id=0, has_side_effects=True, vmem_limit_bytes=40 * 1024 * 1024
+            collective_id=0, has_side_effects=True, vmem_limit_bytes=60 * 1024 * 1024
         ),
     )(
         image[0], margin, cells, weights, observed, dual_start,

time: 54.3 us -> 46.5 us (0.86); the launches traced: 53.6 us -> 46.4 us
  local copies, waits for them, and re-layouts: 11.4 us -> 2.51 us
  Pallas kernels: 40.9 us -> 42.6 us
    unnamed x24 -> x4, local copies, waits for them, and re-layouts: 11.4 us -> 2.51 us
    pallas_call x1, Pallas kernels: 40.9 us -> 42.6 us  [local_kernel(): pl.pallas_call(functools.partial(whole_kernel, n, c), out_shape=(jax.Shap...]
where the time goes in v3:
time: 46.5 us; the launch traced here: 46.4 us
  Pallas kernels  42.6 us (92%)
  local copies, waits for them, and re-layouts  2.51 us (5%)
  between operations  1.29 us (3%)
    pallas_call x1, Pallas kernels, local_kernel(): pl.pallas_call(functools.partial(whole_kernel, n, c), out_shape=(jax.Shap...  42.6 us
    unnamed x4, local copies, waits for them, and re-layouts  2.51 us

profile of v3, /device:TPU:0, one launch (start us, length us, event | category | flops | bytes accessed | tf_op | source)
XLA Modules:
  0.0 46.4 jit_solution(3558401881961968515)
XLA Ops:
  1.3 42.6 %shard_map.131 = (f32[128,1024]{1,0:T(8,128)}, f32[2,1,4096]{2,1,0:T(1,128)}) custom-call(f32[128,1024]{1,0:T(8,128)} %bitcast.3, s32[1]{0:T(128)S(6)} %copy.16.margin_far, s32[1,4096]{1,0:T(1,128)} %cells_far.1, f32[1,4096]{1,0:T(1,128)} %gains_far.1, f32[2,1,4096]{2,1,0:T(1,128)} %seen_far.1, f32[2,1,4096]{2,1,0:T(1,128)} %dual_far.1, ...), custom_call_target="tpu_custom_call" | custom-call | tf_op jit(solution)/shard_map/pallas_call | solution.py:552
  43.8 0.0 copy-start
  43.8 1.9 %copy.17 = f32[1,128,1024]{2,1,0:T(8,128)} copy(f32[1,128,1024]{2,1,0:T(8,128)} %bitcast.2) | data formatting | bytes 1048576
  45.7 0.0 copy-done
  45.7 0.6 %copy.18 = f32[2,1,4096]{2,1,0:T(1,128)} copy(f32[2,1,4096]{2,1,0:T(1,128)S(1)} %copy-done) | data formatting | bytes 65536
Async XLA Ops:
  43.8 1.9 %copy-start = (f32[2,1,4096]{2,1,0:T(1,128)S(1)}, f32[2,1,4096]{2,1,0:T(1,128)}, u32[]{:S(2)}) copy-start(f32[2,1,4096]{2,1,0:T(1,128)} %get-tuple-element.9) | copy-start | bytes 98308

commit v4 on v2

--- a/solution.py
+++ b/solution.py
@@ -455,9 +455,14 @@
         grid[h] = jnp.concatenate(split(values), axis=0)
         lax.fori_loop(0, vis // CHUNK, (visit_first, visit_last)[h], 0, unroll=2)
 
-    hold[...] = lax.dot_general(
-        hot[...], marks[...], crossed, preferred_element_type=jnp.float32
-    ).astype(jnp.bfloat16)
+    def collect(i, carry):
+        here = pl.ds(pl.multiple_of(i * pair, pair), pair)
+        hold[here, :] = lax.dot_general(
+            hot[here, :], marks[...], crossed, preferred_element_type=jnp.float32
+        ).astype(jnp.bfloat16)
+        return carry
+
+    lax.fori_loop(0, width // pair, collect, 0)
 
     sends2 = []
     for d in range(n - 1, -1, -1):
@@ -573,7 +578,7 @@
             dma((c,)), dma((c,)), dma((2,)), dma((2,)),
         ],
         compiler_params=pltpu.CompilerParams(
-            collective_id=0, has_side_effects=True, vmem_limit_bytes=40 * 1024 * 1024
+            collective_id=0, has_side_effects=True, vmem_limit_bytes=60 * 1024 * 1024
         ),
     )(
         image[0], margin, cells, weights, observed, dual_start,

time: 54.3 us -> 45.6 us (0.84)
  local copies, waits for them, and re-layouts: 11.4 us -> 2.51 us
  Pallas kernels: 40.9 us -> 41.6 us
    unnamed x24 -> x4, local copies, waits for them, and re-layouts: 11.4 us -> 2.51 us
    pallas_call x1, Pallas kernels: 40.9 us -> 41.6 us  [local_kernel(): pl.pallas_call(functools.partial(whole_kernel, n, c), out_shape=(jax.Shap...]
where the time goes in v4:
time: 45.6 us; the launch traced here: 45.4 us
  Pallas kernels  41.6 us (91%)
  local copies, waits for them, and re-layouts  2.51 us (6%)
  between operations  1.29 us (3%)
    pallas_call x1, Pallas kernels, local_kernel(): pl.pallas_call(functools.partial(whole_kernel, n, c), out_shape=(jax.Shap...  41.6 us
    unnamed x4, local copies, waits for them, and re-layouts  2.51 us

profile of v4, /device:TPU:0, one launch (start us, length us, event | category | flops | bytes accessed | tf_op | source)
XLA Modules:
  0.0 45.4 jit_solution(5306524669212861934)
XLA Ops:
  1.3 41.6 %shard_map.131 = (f32[128,1024]{1,0:T(8,128)}, f32[2,1,4096]{2,1,0:T(1,128)}) custom-call(f32[128,1024]{1,0:T(8,128)} %bitcast.3, s32[1]{0:T(128)S(6)} %copy.16.margin, s32[1,4096]{1,0:T(1,128)} %cells.1, f32[1,4096]{1,0:T(1,128)} %gains.1, f32[2,1,4096]{2,1,0:T(1,128)} %seen.1, f32[2,1,4096]{2,1,0:T(1,128)} %dual.1, f32[2,1024,128]{2,1,0:T(8,128)} %constant.12.clone.base, ...), custom_call_target="tpu_custom_call" | custom-call | tf_op jit(solution)/shard_map/pallas_call | solution.py:542
  42.9 0.0 copy-start
  42.9 1.9 %copy.17 = f32[1,128,1024]{2,1,0:T(8,128)} copy(f32[1,128,1024]{2,1,0:T(8,128)} %bitcast.2) | data formatting | bytes 1048576
  44.8 0.0 copy-done
  44.8 0.6 %copy.18 = f32[2,1,4096]{2,1,0:T(1,128)} copy(f32[2,1,4096]{2,1,0:T(1,128)S(1)} %copy-done) | data formatting | bytes 65536
Async XLA Ops:
  42.9 1.9 %copy-start = (f32[2,1,4096]{2,1,0:T(1,128)S(1)}, f32[2,1,4096]{2,1,0:T(1,128)}, u32[]{:S(2)}) copy-start(f32[2,1,4096]{2,1,0:T(1,128)} %get-tuple-element.9) | copy-start | bytes 98308
